TPU v7x, 32 devices: a whole 2x2x4 slice. The times are simulated.
32 devices in a mesh: batch: 4 (over y, x), seq: 2 (over core), tp: 4 (over z).
Axes of the slice: x: 2, y: 2, z: 4, core: 2. Of those that a mesh axis runs over, the one named last changes fastest.
Arguments:
- values: bfloat16 [8192, 8192], P(('batch', 'seq'), 'tp'), parts along dimension 0, may hold values from -6 to 6
- gate_in: bfloat16 [8192, 8192], P(('batch', 'seq'), 'tp'), parts along dimension 0, may hold values from -6 to 6
- write_proj: bfloat16 [8192, 1024], P(('batch', 'seq'), 'tp'), parts along dimension 0, may hold values from -0.59765625 to 0.59765625
- read_proj: bfloat16 [8192, 1024], P(('batch', 'seq'), 'tp'), parts along dimension 0, may hold values from -6 to 6
- step_size: float32 [8192, 64], P(('batch', 'seq'), 'tp'), parts along dimension 0, may hold values from 0.02 to 0.2
- log_gate: float32 [8192, 64], P(('batch', 'seq'), 'tp'), parts along dimension 0, may hold values from -4.5 to 0, as said below
- skip_gain: float32 [64], P('tp'), may hold values from 0.5 to 4
- norm_gain: bfloat16 [8192], P('tp'), may hold values from 0.5 to 1.5
- history: float32 [256, 128, 128], P(('batch', 'tp')), parts along dimension 0, may hold values from -6 to 6
Outputs:
- normed: bfloat16 [8192, 8192], P(('batch', 'seq'), 'tp'), parts along dimension 0
- final_state: float32 [256, 128, 128], P(('batch', 'tp'), 'seq'), parts along dimension 0
There are 4 independent parts, one for each index of `batch`. A program takes and returns all parts, laid end to end along the dimension named above; an argument that names none is the same for every part. Nothing has to cross between parts.
Inputs may be any that keep to these rules, and one draw needn't show every extreme that they name: `log_gate`: negative everywhere.
All inputs are finite; a program needn't handle non-finite values.
Results may differ from a plain program's by a relative error of at most 0.001.
Values sent between devices are 32-bit elements; how exact they have to be, the bound alone decides.
A program may use at most 128 MiB of HBM per device.

v0:
```python
import math

import jax
import jax.numpy as jnp
from jax import lax
from jax.sharding import PartitionSpec as P

highest = lax.Precision.HIGHEST


def shifted(array, axis, by):
    peers = lax.axis_size(axis)
    pairs = [(i, i + by) for i in range(peers) if 0 <= i + by < peers]
    return lax.ppermute(array, axis, pairs)


def from_root(array, axis, root):
    mine = lax.axis_index(axis) == root
    return lax.psum(jnp.where(mine, array, jnp.zeros_like(array)), axis)


def combine_pair(earlier, later):
    return (earlier[0] + later[0], jnp.exp(later[0])[..., None, None] * earlier[1] + later[1])


def body(
    values, gate_in, write_proj, read_proj, step_size, log_gate, skip_gain, norm_gain, history
):
    heads = skip_gain.shape[0]
    head_size = history.shape[1]
    memory_dimension = history.shape[2]
    groups = write_proj.shape[1] // memory_dimension
    per_group = heads // groups
    rows = values.shape[0]
    block = math.gcd(rows, 256)
    blocks = rows // block
    inputs_flat = values.astype(jnp.float32)
    inputs_all = inputs_flat.reshape(blocks, block, groups, per_group, head_size)
    write_wide = write_proj.astype(jnp.float32)
    read_wide = read_proj.astype(jnp.float32)
    write_all = write_wide.reshape(blocks, block, groups, memory_dimension)
    read_all = read_wide.reshape(blocks, block, groups, memory_dimension)
    steps_all = step_size.reshape(blocks, block, groups, per_group)
    gates_all = log_gate.reshape(blocks, block, groups, per_group)
    cumul = jnp.cumsum(gates_all, axis=1)
    cumul_heads = jnp.transpose(cumul, (0, 2, 3, 1))
    steps_heads = jnp.transpose(steps_all, (0, 2, 3, 1))
    scores = jnp.einsum("btgn,bsgn->bgts", read_all, write_all, precision=highest)
    diffs = cumul_heads[..., :, None] - cumul_heads[..., None, :]
    causal = jnp.arange(block)[:, None] >= jnp.arange(block)[None, :]
    decay = jnp.exp(jnp.where(causal, diffs, -jnp.inf))
    weights = scores[:, :, None] * decay * steps_heads[:, :, :, None, :]
    inside = jnp.einsum("bgkts,bsgkp->btgkp", weights, inputs_all, precision=highest)
    last_sum = cumul[:, -1]
    tail_weight = jnp.exp(last_sum[:, None] - cumul) * steps_all
    scaled = tail_weight[..., None] * inputs_all
    deltas = jnp.einsum("btgkp,btgn->bgkpn", scaled, write_all, precision=highest)
    empty_state = jnp.zeros((groups, per_group, head_size, memory_dimension), jnp.float32)
    zero_decay = jnp.zeros((groups, per_group), jnp.float32)
    local_state = empty_state
    local_decay = zero_decay
    starts_list = []
    offsets_list = []
    for index_blk in range(blocks):
        starts_list.append(local_state)
        offsets_list.append(local_decay)
        local_state = (
            jnp.exp(last_sum[index_blk])[..., None, None] * local_state + deltas[index_blk]
        )
        local_decay = local_decay + last_sum[index_blk]
    starts = jnp.stack(starts_list)
    offsets = jnp.stack(offsets_list)
    earlier = jnp.exp(cumul)[..., None] * jnp.einsum(
        "bgkpn,btgn->btgkp", starts, read_all, precision=highest
    )
    partial_value = (inside + earlier).reshape(rows, groups, per_group, head_size)
    running = (cumul + offsets[:, None]).reshape(rows, groups, per_group)

    def forward(turn_id, carried):
        joined = combine_pair(carried, (local_decay, local_state))
        return shifted((joined[0], joined[1]), "seq", 1)

    prefix = lax.fori_loop(0, lax.axis_size("seq") - 1, forward, (zero_decay, empty_state))
    start = history.reshape(groups, per_group, head_size, memory_dimension)
    entering = jnp.exp(prefix[0])[..., None, None] * start + prefix[1]
    read_rows = read_wide.reshape(rows, groups, memory_dimension)
    correction = jnp.exp(running)[..., None] * jnp.einsum(
        "gkpn,tgn->tgkp", entering, read_rows, precision=highest
    )
    inputs_rows = inputs_flat.reshape(rows, groups, per_group, head_size)
    outputs = (
        partial_value
        + correction
        + skip_gain.reshape(groups, per_group)[None, :, :, None] * inputs_rows
    )
    gated = outputs * jax.nn.silu(
        gate_in.astype(jnp.float32).reshape(rows, groups, per_group, head_size)
    )
    meansq = jnp.mean(gated * gated, axis=(2, 3), keepdims=True)
    result = (
        gated
        * lax.rsqrt(meansq + 1e-05)
        * norm_gain.astype(jnp.float32).reshape(1, groups, per_group, head_size)
    )
    normed = result.reshape(rows, heads * head_size).astype(jnp.bfloat16)
    sequence_count = lax.axis_size("seq")
    share = head_size // sequence_count
    closing_index = jnp.exp(local_decay)[..., None, None] * entering + local_state
    whole = from_root(closing_index, "seq", sequence_count - 1)
    final_state = lax.dynamic_slice_in_dim(whole, lax.axis_index("seq") * share, share, 2).reshape(
        heads, share, memory_dimension
    )
    return (normed, final_state)


def solution(mesh):
    return jax.shard_map(
        body,
        mesh=mesh,
        in_specs=(
            P(("batch", "seq"), "tp"),
            P(("batch", "seq"), "tp"),
            P(("batch", "seq"), "tp"),
            P(("batch", "seq"), "tp"),
            P(("batch", "seq"), "tp"),
            P(("batch", "seq"), "tp"),
            P("tp"),
            P("tp"),
            P(("batch", "tp"), None, None),
        ),
        out_specs=(P(("batch", "seq"), "tp"), P(("batch", "tp"), "seq", None)),
        check_vma=False,
    )
```

profile of v0, /device:TPU:0, one launch (start us, length us, event | category | flops | bytes accessed | tf_op | source)
XLA Modules:
  0.0 144.6 jit_solution(8302489780493218628)
XLA Ops:
  7.2 0.0 all-reduce.2.cloned.1.call-start
  7.2 0.8 copy_bitcast_fusion
  8.1 4.5 %reduce-window.6 = f32[4,8,2,2,128]{4,1,2,3,0:T(8,128)S(1)} reduce-window(f32[4,8,2,2,128]{4,1,2,3,0:T(8,128)S(1)} %copy_bitcast_fusion, f32[]{:T(128)} %constant.11.clone.1), window={size=1x1x1x1x128 pad=0_0x0_0x0_0x0_0x127_0}, to_apply=%region_0.0 | reduce-window | flops 2080768 | bytes 131076 | tf_op jit(solution)/shard_map/reduce-window
  12.6 0.1 slice.59
  12.6 0.2 copy.49
  12.8 0.1 bitcast_bitcast_fusion
  12.9 0.2 add_reduce_fusion
  13.1 2.4 %collective-permute-start = (f32[2,8]{1,0:T(2,128)S(1)}, f32[2,8]{1,0:T(2,128)S(1)}, u32[]{:S(2)}, u32[]{:S(2)}) collective-permute-start(f32[2,8]{1,0:T(2,128)S(1)} %get-tuple-element.23), channel_id=1, source_target_pairs={{0,4},{1,5},{2,6},{3,7},{8,12},{9,13},{10,14},{11,15},{16,20},{17,... | collective-permute-start | bytes 200 | tf_op jit(solution)/shard_map/while/body/eval_jaxpr/ppermute | solution.py:14
  15.5 0.2 slice_reduce_fusion
  15.6 0.9 reshape.177
  16.5 1.2 reshape.173
  17.7 3.2 %convert_bitcast_fusion = f32[128,8,16,128]{3,1,2,0:T(8,128)S(1)} fusion(bf16[1024,2048]{1,0:T(8,128)(2,1)} %param.9), kind=kLoop, calls=%fused_computation.32 | loop fusion | flops 2097152 | bytes 12582912
  20.9 5.2 %copy.80 = f32[128,8,16,128]{3,2,1,0:T(8,128)} copy(f32[128,8,16,128]{3,1,2,0:T(8,128)S(1)} %convert_bitcast_fusion) | data formatting | bytes 16777216
  26.1 9.9 %copy.55 = f32[4,256,2,8,128]{1,4,3,2,0:T(8,128)} copy(f32[4,256,2,8,128]{4,3,2,1,0:T(8,128)} %bitcast.110) | data formatting | bytes 16777216 | tf_op jit(solution)/shard_map/reshape | solution.py:38
  36.1 0.1 pad_maximum_fusion
  36.2 0.1 exponential_bitcast_fusion
  36.3 0.0 copy-start.2
  36.3 6.5 %fusion.10 = f32[4,2,8,128,128]{4,3,2,1,0:T(8,128)S(1)} fusion(f32[4,256,2,8,128]{1,4,3,2,0:T(8,128)} %copy.55, f32[4,256,2,8]{1,3,2,0:T(8,128)S(1)} %get-tuple-element.40, bf16[4,256,2,128,1]{3,2,1,0,4:T(2,128)(2,1)S(1)} %bitcast.115), kind=kOutput, calls=%fused_computation.14 | convolution fusion | flops 3223322624 | bytes 13172736 | tf_op jit(solution)/shard_map/btgkp,btgn->bgkpn/dot_general | solution.py:57
  42.8 0.0 copy-start
  42.8 2.0 %copy-done = f32[4,2,8,128,128]{4,3,2,1,0:T(8,128)} copy-done((f32[4,2,8,128,128]{4,3,2,1,0:T(8,128)}, f32[4,2,8,128,128]{4,3,2,1,0:T(8,128)S(1)}, u32[]{:S(2)}) %copy-start) | copy-done | bytes 4194328
  44.8 1.4 broadcast_add_fusion
  46.2 2.4 %collective-permute-start.1 = (f32[2,8,128,128]{3,2,1,0:T(8,128)}, f32[2,8,128,128]{3,2,1,0:T(8,128)}, u32[]{:S(2)}, u32[]{:S(2)}) collective-permute-start(f32[2,8,128,128]{3,2,1,0:T(8,128)} %get-tuple-element.31), channel_id=1, source_target_pairs={{0,4},{1,5},{2,6},{3,7},{8,12},{9,13},{10,14},{11,15},{16,20},{17,... | collective-permute-start | bytes 3145736 | tf_op jit(solution)/shard_map/while/body/eval_jaxpr/ppermute | solution.py:14
  48.6 0.0 copy-done.2
  48.6 0.1 reshape.172
  48.8 0.4 fusion.37
  49.2 3.6 %copy.79 = bf16[128,8,16,128]{3,2,1,0:T(8,128)(2,1)S(1)} copy(bf16[128,8,16,128]{3,1,2,0:T(8,128)(2,1)} %bitcast.109) | data formatting | bytes 8388608
  52.8 0.0 copy-start.1
  52.8 13.8 %fusion = f32[4,2,8,256,128]{4,3,2,1,0:T(8,128)} fusion(f32[4,2,8,256]{3,2,1,0:T(8,128)S(1)} %copy.52, f32[4,2,8,256]{3,2,1,0:T(8,128)S(1)} %get-tuple-element.42, f32[4,2,256,256]{3,2,1,0:T(8,128)S(1)} %fusion.37, pred[256,256]{1,0:T(8,128)(4,1)S(1)} %iota_compare_fusion, bf16[4,256,2,8,128]{4,3,2,1,0:T(8,128)(2,1)S(1)} %bitcast.117), kind=kOutput, calls=%fused_computation | convolution fusion | flops 6459228160 | bytes 14876672 | tf_op jit(solution)/shard_map/bgkts,bsgkp->btgkp/dot_general | solution.py:53
  66.6 0.0 copy-done.1
  66.6 1.7 %multiply_add_fusion.1 = (f32[1,2,8,128,128]{4,3,2,1,0:T(8,128)S(1)}, f32[1,2,8,128,128]{4,3,2,1,0:T(8,128)}, f32[1,2,8,128,128]{4,3,2,1,0:T(8,128)}) fusion(f32[4,2,8,128,128]{4,3,2,1,0:T(8,128)S(1)} %copy-done.1, f32[2,8]{1,0:T(2,128)S(1)} %get-tuple-element.26, f32[2,8]{1,0:T(2,128)S(1)} %get-tuple-element.27, f32[2,8]{1,0:T(2,128)S(1)} %get-tuple-element.29), kind=kLoop, calls=%fused_computation.43 | loop fusion | flops 1310720 | bytes 6291648 | tf_op jit(solution)/shard_map/add | solution.py:68
  68.3 6.9 %copy.63 = f32[1024,2048]{0,1:T(8,128)} copy(bf16[1024,2048]{1,0:T(8,128)(2,1)} %param.9) | data formatting | bytes 12582912 | tf_op jit(solution)/shard_map/convert_element_type | solution.py:37
  75.2 0.9 reshape.182
  76.1 7.7 %fusion.9 = f32[4,256,2,8,128]{4,1,3,2,0:T(8,128)S(1)} fusion(f32[4,2,8,256,128]{4,3,2,1,0:T(8,128)} %fusion, f32[4,256,2,8]{1,3,2,0:T(8,128)S(1)} %get-tuple-element.39, f32[1,2,8,128,128]{4,3,2,1,0:T(8,128)S(1)} %get-tuple-element.35, f32[1,2,8,128,128]{4,3,2,1,0:T(8,128)} %get-tuple-element.36, f32[1,2,8,128,128]{4,3,2,1,0:T(8,128)} %get-tuple-element.37, ...), kind=kOutput, calls=%fused_computation.11 | convolution fusion | flops 3228565504 | bytes 20512784 | tf_op jit(solution)/shard_map/bgkpn,btgn->btgkp/dot_general | solution.py:73
  83.8 8.1 %copy.59 = f32[4,256,2,8,128]{4,3,2,1,0:T(8,128)} copy(f32[4,256,2,8,128]{4,1,3,2,0:T(8,128)S(1)} %fusion.9) | data formatting | bytes 16777216 | tf_op jit(solution)/shard_map/add | solution.py:76
  91.9 8.7 %copy.62 = f32[1024,2,8,128]{0,3,2,1:T(8,128)} copy(f32[1024,2,8,128]{3,2,1,0:T(8,128)} %bitcast.111) | data formatting | bytes 16777216 | tf_op jit(solution)/shard_map/reshape | solution.py:76
  100.7 0.0 copy-start.5
  100.7 7.0 %copy.64 = f32[1024,2048]{0,1:T(8,128)} copy(bf16[1024,2048]{1,0:T(8,128)(2,1)} %param.10) | data formatting | bytes 12582912 | tf_op jit(solution)/shard_map/reshape | solution.py:97
  107.7 0.0 copy-done.7
  107.7 0.1 mul.194
  107.8 0.0 collective-permute-done
  107.8 0.0 collective-permute-done.1
  107.8 2.5 %add_select_fusion = f32[2,8,128,128]{3,2,1,0:T(8,128)} fusion(f32[2,8,128,128]{3,2,1,0:T(8,128)S(1)} %get-tuple-element.32, f32[2,8]{1,0:T(2,128)S(1)} %get-tuple-element.43, pred[]{:T(512)S(6)} %eq.3, f32[2,8,128,128]{3,2,1,0:T(8,128)} %collective-permute-done.1, f32[2,8]{1,0:T(2,128)S(1)} %exp.83, f32[16,128,128]{2,1,0:T(8,128)S(1)} %copy-done.4), kind=kLoop, calls=%fused_computation.41 | loop fusion | flops 1310720 | bytes 4194433 | tf_op jit(solution)/shard_map/jit(_where)/select_n | solution.py:19
  110.3 0.0 all-reduce.2.cloned.1.call-update
  110.3 0.0 copy-done.5
  110.3 16.6 %multiply_reduce_fusion = (f32[1024,2]{0,1:T(2,128)S(1)}, f32[1024,2,8,128]{0,3,2,1:T(8,128)S(1)}) fusion(f32[1024,2,8,128]{0,3,2,1:T(8,128)} %bitcast.114, f32[1024,2,8,128]{0,3,2,1:T(8,128)} %bitcast.113, f32[2,8]{1,0:T(2,128)S(1)} %mul.194, f32[1024,2,8,128]{0,3,2,1:T(8,128)} %copy.62, bf16[1024,2,128,1]{2,1,0,3:T(2,128)(2,1)S(1)} %bitcast.120, ...), kind=kOutput, calls=%fused_computation.13 | convolution fusion | flops 3244816384 | bytes 36249728 | tf_op jit(solution)/shard_map/gkpn,tgn->tgkp/dot_general | solution.py:87
  127.0 2.4 %multiply_convert_fusion = bf16[1024,2,8,128]{0,3,2,1:T(8,128)(2,1)} fusion(f32[1024,2,8,128]{0,3,2,1:T(8,128)S(1)} %get-tuple-element.46, f32[2,8,128]{2,1,0:T(8,128)S(1)} %bitcast_convert_fusion, f32[1024,2]{0,1:T(2,128)S(1)} %add_rsqrt_fusion), kind=kLoop, calls=%fused_computation.12 | loop fusion | flops 6291456 | bytes 12599296 | tf_op jit(solution)/shard_map/convert_element_type | solution.py:105
  129.4 6.5 %copy.65 = bf16[1024,2048]{1,0:T(8,128)(2,1)} copy(bf16[1024,2048]{0,1:T(8,128)(2,1)} %bitcast.112) | data formatting | bytes 8388608
  135.8 1.9 %constant_dynamic-slice_fusion = f32[2,8,64,128]{3,2,1,0:T(8,128)} fusion(f32[2,8,128,128]{3,2,1,0:T(8,128)} %all-reduce.2.cloned.1.call-done, s32[]{:T(128)S(6)} %select_n.18), kind=kLoop, calls=%fused_computation.78 | loop fusion | bytes 1048580 | tf_op jit(solution)/shard_map/dynamic_slice | solution.py:110
  (20 shorter events, 0.1 us)
Async XLA Ops:
  7.2 128.7 %all-reduce.2.cloned.1.call-start = ((), (), s32[]{:S(2)}) async-start(), calls=%async_computation | async-start | bytes 2097152 | tf_op jit(solution)/shard_map/psum | solution.py:19
  13.1 94.7 %collective-permute-start = (f32[2,8]{1,0:T(2,128)S(1)}, f32[2,8]{1,0:T(2,128)S(1)}, u32[]{:S(2)}, u32[]{:S(2)}) collective-permute-start(f32[2,8]{1,0:T(2,128)S(1)} %get-tuple-element.23), channel_id=1, source_target_pairs={{0,4},{1,5},{2,6},{3,7},{8,12},{9,13},{10,14},{11,15},{16,20},{17,... | collective-permute-start | bytes 200 | tf_op jit(solution)/shard_map/while/body/eval_jaxpr/ppermute | solution.py:14
  36.3 12.3 %copy-start.2 = (bf16[1024,256]{1,0:T(8,128)(2,1)S(1)}, bf16[1024,256]{1,0:T(8,128)(2,1)}, u32[]{:S(2)}) copy-start(bf16[1024,256]{1,0:T(8,128)(2,1)} %param.12) | copy-start | bytes 1572868
  42.8 2.0 %copy-start = (f32[4,2,8,128,128]{4,3,2,1,0:T(8,128)}, f32[4,2,8,128,128]{4,3,2,1,0:T(8,128)S(1)}, u32[]{:S(2)}) copy-start(f32[4,2,8,128,128]{4,3,2,1,0:T(8,128)S(1)} %fusion.10) | copy-start | bytes 12582916
  46.2 61.6 %collective-permute-start.1 = (f32[2,8,128,128]{3,2,1,0:T(8,128)}, f32[2,8,128,128]{3,2,1,0:T(8,128)}, u32[]{:S(2)}, u32[]{:S(2)}) collective-permute-start(f32[2,8,128,128]{3,2,1,0:T(8,128)} %get-tuple-element.31), channel_id=1, source_target_pairs={{0,4},{1,5},{2,6},{3,7},{8,12},{9,13},{10,14},{11,15},{16,20},{17,... | collective-permute-start | bytes 3145736 | tf_op jit(solution)/shard_map/while/body/eval_jaxpr/ppermute | solution.py:14
  52.8 13.8 %copy-start.1 = (f32[4,2,8,128,128]{4,3,2,1,0:T(8,128)S(1)}, f32[4,2,8,128,128]{4,3,2,1,0:T(8,128)}, u32[]{:S(2)}) copy-start(f32[4,2,8,128,128]{4,3,2,1,0:T(8,128)} %copy-done) | copy-start | bytes 12582916
  66.6 8.6 %copy-start.3 = (bf16[1024,256]{1,0:T(8,128)(2,1)S(1)}, bf16[1024,256]{1,0:T(8,128)(2,1)}, u32[]{:S(2)}) copy-start(bf16[1024,256]{1,0:T(8,128)(2,1)} %param.12) | copy-start | bytes 1572868
  100.7 7.0 %copy-start.7 = (f32[16]{0:T(128)S(1)}, f32[16]{0:T(128)}, u32[]{:S(2)}) copy-start(f32[16]{0:T(128)} %param.15) | copy-start | bytes 196
  100.7 7.1 %copy-start.6 = (bf16[2048]{0:T(1024)(128)(2,1)S(1)}, bf16[2048]{0:T(1024)(128)(2,1)}, u32[]{:S(2)}) copy-start(bf16[2048]{0:T(1024)(128)(2,1)} %param.16) | copy-start | bytes 12292
  100.7 7.1 %copy-start.4 = (f32[16,128,128]{2,1,0:T(8,128)S(1)}, f32[16,128,128]{2,1,0:T(8,128)}, u32[]{:S(2)}) copy-start(f32[16,128,128]{2,1,0:T(8,128)} %param.17) | copy-start | bytes 3145732
  100.7 9.6 %copy-start.5 = (bf16[1024,2,128]{2,1,0:T(2,128)(2,1)S(1)}, bf16[1024,2,128]{2,1,0:T(2,128)(2,1)}, u32[]{:S(2)}) copy-start(bf16[1024,2,128]{2,1,0:T(2,128)(2,1)} %reshape.182) | copy-start | bytes 1572868
Sparse Core Ops, SparseCore 0:
  110.4 21.6 all-reduce.1
where the time goes:
time: 146 us; the launch traced here: 145 us
  local copies, waits for them, and re-layouts  64.3 us (44%)
  matrix products  45.1 us (31%)
  other arithmetic  16.2 us (11%)
  between operations  14.2 us (10%)
  starting transfers between devices  4.75 us (3%)
    unnamed x19, local copies, waits for them, and re-layouts  17.3 us
    dot_general x1, matrix products, body(): jnp.einsum('gkpn,tgn->tgkp', entering, read_rows, precision=highest)  16.6 us
    dot_general x1, matrix products, body(): jnp.einsum('bgkts,bsgkp->btgkp', weights, inputs_all, precision=highest)  13.8 us
    reshape x1, local copies, waits for them, and re-layouts, body(): inputs_flat.reshape(blocks, block, groups, per_group, head_size)  9.94 us
    reshape x1, local copies, waits for them, and re-layouts, body(): (inside + earlier).reshape(rows, groups, per_group, head_size)  8.74 us
    add x1, local copies, waits for them, and re-layouts, body(): inside + earlier  8.08 us
    dot_general x1, matrix products, body(): jnp.einsum('bgkpn,btgn->btgkp', starts, read_all, precision=highest)  7.74 us
    reshape x1, local copies, waits for them, and re-layouts, body(): gate_in.astype(jnp.float32).reshape(rows, groups, per_group, head_size)  6.99 us
  transfers between devices with their start and end apart: 3, of which 0 were waited for; matrix products, arithmetic and copies ran while one was open for 78% of the time, Pallas kernels for 0%

commit v1 on v0

v1 whole, which is shorter than its diff:
```python
import functools
import math

import jax
import jax.numpy as jnp
from jax import lax
from jax.experimental import pallas as pl
from jax.experimental.pallas import tpu as pltpu
from jax.sharding import PartitionSpec as P

HIGH = lax.Precision.HIGHEST
LOG2E = math.log2(math.e)
MESH = pl.DeviceIdType.MESH
F32 = jnp.float32
BF16 = jnp.bfloat16


def upper(size):
    rows = lax.broadcasted_iota(jnp.int32, (size, size), 0)
    cols = lax.broadcasted_iota(jnp.int32, (size, size), 1)
    return rows <= cols


def split(value):
    high = value.astype(BF16)
    low = (value - high.astype(F32)).astype(BF16)
    return high, low


def turned(array, matrix):
    return lax.dot_general(
        array, matrix, (((0,), (0,)), ((), ())), precision=HIGH, preferred_element_type=F32
    )


def rows_of(gates, steps):
    size = gates.shape[0]
    ones = upper(size).astype(F32)
    rows = lax.broadcasted_iota(jnp.int32, (size, size), 0)
    cols = lax.broadcasted_iota(jnp.int32, (size, size), 1)
    eye = (rows == cols).astype(F32)
    cumul = turned(gates * LOG2E, ones)
    shift = cumul - turned(jnp.log2(steps), eye)
    last = cumul[:, size - 1 : size]
    return shift, last


def chain_kernel(
    peers, x_ref, b_ref, step_ref, gate_ref, hist_ref, ent_ref, fin_ref,
    state, total, recv, send, full, fin_recv, send_sem, recv_sem, fin_send_sem, fin_recv_sem,
):
    group, blk = pl.program_id(0), pl.program_id(1)
    groups, blocks = pl.num_programs(0), pl.num_programs(1)
    count = recv.shape[0]
    me = lax.axis_index("seq")
    size = b_ref.shape[0]
    width = b_ref.shape[1]
    heads = hist_ref.shape[0]
    per_group = heads // count
    share = fin_ref.shape[1]

    @pl.when((group == 0) & (blk == 0))
    def _():
        barrier = pltpu.get_barrier_semaphore()
        for by in range(1, peers):
            other = lax.rem(me + by, peers)
            pl.semaphore_signal(barrier, inc=1, device_id={"seq": other}, device_id_type=MESH)
        pl.semaphore_wait(barrier, peers - 1)

    shift, last = rows_of(gate_ref[...], step_ref[...])
    tails = jnp.exp2(last - shift)
    decays = jnp.exp2(jnp.broadcast_to(last, (heads, width)))
    turned_b = jnp.transpose(b_ref[...].astype(F32))

    @pl.when(blk == 0)
    def _():
        state[...] = jnp.zeros_like(state)
        total[...] = jnp.zeros_like(total)

    total[...] += jnp.broadcast_to(last, (heads, width))

    def update(first):
        for k in range(per_group):
            h = first + k
            cols = slice(k * width, (k + 1) * width)
            high, low = split(turned_b * tails[h : h + 1, :])
            x = x_ref[:, cols]
            delta = jnp.dot(high, x, preferred_element_type=F32) + jnp.dot(
                low, x, preferred_element_type=F32
            )
            state[:, cols] = decays[h : h + 1, :] * state[:, cols] + delta

    def joined(k, h, entering):
        cols = slice(k * width, (k + 1) * width)
        return jnp.exp2(total[h : h + 1, :]) * entering + state[:, cols]

    def link(g):
        return pltpu.make_async_remote_copy(
            src_ref=send.at[g], dst_ref=recv.at[g],
            send_sem=send_sem.at[g], recv_sem=recv_sem.at[g],
            device_id={"seq": jnp.minimum(me + 1, peers - 1)}, device_id_type=MESH,
        )

    for g in range(count):

        @pl.when(group == g)
        def _(g=g):
            update(g * per_group)

            @pl.when(blk == blocks - 1)
            def _():
                for k in range(per_group):
                    h = g * per_group + k
                    cols = slice(k * width, (k + 1) * width)
                    send[g, :, cols] = state[:, cols]

            @pl.when((blk == blocks - 1) & (me == 0))
            def _():
                for k in range(per_group):
                    h = g * per_group + k
                    cols = slice(k * width, (k + 1) * width)
                    entering = jnp.transpose(hist_ref[h])
                    ent_ref[g, :, cols] = entering
                    send[g, :, cols] = joined(k, h, entering)
                link(g).start()

    @pl.when((group == groups - 1) & (blk == blocks - 1))
    def _():
        def to_peer(d):
            return pltpu.make_async_remote_copy(
                src_ref=full.at[d], dst_ref=fin_recv,
                send_sem=fin_send_sem.at[d], recv_sem=fin_recv_sem,
                device_id={"seq": d}, device_id_type=MESH,
            )

        @pl.when(me > 0)
        def _():
            for g in range(count):
                link(g).wait_recv()
                for k in range(per_group):
                    h = g * per_group + k
                    cols = slice(k * width, (k + 1) * width)
                    entering = recv[g, :, cols]
                    ent_ref[g, :, cols] = entering
                    send[g, :, cols] = jnp.exp2(total[h : h + 1, :]) * entering + send[g, :, cols]

                @pl.when(me < peers - 1)
                def _(g=g):
                    link(g).start()

        @pl.when(me == peers - 1)
        def _():
            for g in range(count):
                for k in range(per_group):
                    h = g * per_group + k
                    cols = slice(k * width, (k + 1) * width)
                    closing = jnp.transpose(send[g, :, cols])
                    for d in range(peers - 1):
                        full[d, h] = closing[d * share : (d + 1) * share]
                    fin_ref[h] = closing[(peers - 1) * share :]
            for d in range(peers - 1):
                to_peer(d).start()
            for d in range(peers - 1):
                to_peer(d).wait_send()

        @pl.when(me < peers - 1)
        def _():
            for g in range(count):
                link(g).wait_send()
            to_peer(0).wait_recv()
            fin_ref[...] = fin_recv[...]


def mix_kernel(
    x_ref, z_ref, b_ref, c_ref, step_ref, gate_ref, skip_ref, gain_ref, ent_ref, out_ref,
    state, parts, gated,
):
    groups, width, span = state.shape
    size = b_ref.shape[0]
    per_group = span // width
    heads = groups * per_group

    @pl.when(pl.program_id(0) == 0)
    def _():
        for g in range(groups):
            for k in range(per_group):
                cols = slice(k * width, (k + 1) * width)
                entering = ent_ref[g, :, cols]
                high, low = split(entering)
                state[g, :, cols] = entering
                parts[g, :width, cols] = high
                parts[g, width:, cols] = low

    gates, steps = gate_ref[...], step_ref[...]
    shift, last = rows_of(gates, steps)
    tails = jnp.exp2(last - shift)
    decays = jnp.exp2(jnp.broadcast_to(last, (heads, width)))
    rows = lax.broadcasted_iota(jnp.int32, (size, size), 0)
    cols_at = lax.broadcasted_iota(jnp.int32, (size, size), 1)
    causal = rows >= cols_at
    cumul = jnp.dot(
        causal.astype(F32), gates * LOG2E, precision=HIGH, preferred_element_type=F32
    )
    for g in range(groups):
        write = b_ref[:, g * width : (g + 1) * width]
        read = c_ref[:, g * width : (g + 1) * width]
        scores = lax.dot_general(
            read, write, (((1,), (1,)), ((), ())), preferred_element_type=F32
        )
        scores = jnp.where(causal, scores, 0.0)
        turned_b = jnp.transpose(write.astype(F32))
        earlier = jnp.dot(
            jnp.concatenate([read, read], axis=1), parts[g], preferred_element_type=F32
        )
        squares = jnp.zeros((size, width), F32)
        for k in range(per_group):
            h = g * per_group + k
            cols = slice(k * width, (k + 1) * width)
            wide = slice(h * width, (h + 1) * width)
            x = x_ref[:, wide]
            along = jnp.broadcast_to(cumul[:, h : h + 1], (size, width))
            weights = scores * jnp.exp2(
                jnp.minimum(jnp.broadcast_to(cumul[:, h : h + 1], (size, size)) - shift[h : h + 1, :], 0.0)
            )
            left = jnp.concatenate(
                [
                    jnp.concatenate(split(weights), axis=1),
                    jnp.concatenate(split(turned_b * tails[h : h + 1, :]), axis=1),
                ],
                axis=0,
            )
            both = jnp.dot(left, jnp.concatenate([x, x], axis=0), preferred_element_type=F32)
            later = decays[h : h + 1, :] * state[g, :, cols] + both[size:]
            high, low = split(later)
            state[g, :, cols] = later
            parts[g, :width, cols] = high
            parts[g, width:, cols] = low
            y = both[:size] + jnp.exp2(along) * earlier[:, cols] + skip_ref[h] * x.astype(F32)
            z = z_ref[:, wide].astype(F32)
            value = y * (0.5 * z * (1.0 + jnp.tanh(0.5 * z)))
            gated[:, cols] = value
            squares = squares + value * value
        mean = jnp.sum(squares, axis=1, keepdims=True) * (1.0 / span)
        scale = jnp.broadcast_to(lax.rsqrt(mean + 1e-05), (size, width))
        for k in range(per_group):
            h = g * per_group + k
            cols = slice(k * width, (k + 1) * width)
            wide = slice(h * width, (h + 1) * width)
            out_ref[:, wide] = (
                gated[:, cols] * scale * gain_ref[:, wide].astype(F32)
            ).astype(BF16)


def body(
    values, gate_in, write_proj, read_proj, step_size, log_gate, skip_gain, norm_gain, history
):
    heads, head_size, width = history.shape
    groups = write_proj.shape[1] // width
    per_group = heads // groups
    span = per_group * head_size
    rows = values.shape[0]
    peers = lax.axis_size("seq")
    share = head_size // peers
    big = math.gcd(rows, 256)
    small = math.gcd(rows, 128)

    entering, final_state = pl.pallas_call(
        functools.partial(chain_kernel, peers),
        grid=(groups, rows // big),
        in_specs=[
            pl.BlockSpec((big, span), lambda g, c: (c, g)),
            pl.BlockSpec((big, width), lambda g, c: (c, g)),
            pl.BlockSpec((big, heads), lambda g, c: (c, 0)),
            pl.BlockSpec((big, heads), lambda g, c: (c, 0)),
            pl.BlockSpec((heads, head_size, width), lambda g, c: (0, 0, 0)),
        ],
        out_specs=[
            pl.BlockSpec((groups, width, span), lambda g, c: (0, 0, 0)),
            pl.BlockSpec((heads, share, width), lambda g, c: (0, 0, 0)),
        ],
        out_shape=[
            jax.ShapeDtypeStruct((groups, width, span), F32),
            jax.ShapeDtypeStruct((heads, share, width), F32),
        ],
        scratch_shapes=[
            pltpu.VMEM((width, span), F32),
            pltpu.VMEM((heads, width), F32),
            pltpu.VMEM((groups, width, span), F32),
            pltpu.VMEM((groups, width, span), F32),
            pltpu.VMEM((peers - 1, heads, share, width), F32),
            pltpu.VMEM((heads, share, width), F32),
            pltpu.SemaphoreType.DMA((groups,)),
            pltpu.SemaphoreType.DMA((groups,)),
            pltpu.SemaphoreType.DMA((peers - 1,)),
            pltpu.SemaphoreType.DMA,
        ],
        compiler_params=pltpu.CompilerParams(
            collective_id=0, has_side_effects=True, vmem_limit_bytes=40 << 20
        ),
        name="chain",
    )(values, write_proj, step_size, log_gate, history)

    normed = pl.pallas_call(
        mix_kernel,
        grid=(rows // small,),
        in_specs=[
            pl.BlockSpec((small, heads * head_size), lambda c: (c, 0)),
            pl.BlockSpec((small, heads * head_size), lambda c: (c, 0)),
            pl.BlockSpec((small, groups * width), lambda c: (c, 0)),
            pl.BlockSpec((small, groups * width), lambda c: (c, 0)),
            pl.BlockSpec((small, heads), lambda c: (c, 0)),
            pl.BlockSpec((small, heads), lambda c: (c, 0)),
            pl.BlockSpec(memory_space=pltpu.SMEM),
            pl.BlockSpec((1, heads * head_size), lambda c: (0, 0)),
            pl.BlockSpec((groups, width, span), lambda c: (0, 0, 0)),
        ],
        out_specs=pl.BlockSpec((small, heads * head_size), lambda c: (c, 0)),
        out_shape=jax.ShapeDtypeStruct((rows, heads * head_size), BF16),
        scratch_shapes=[
            pltpu.VMEM((groups, width, span), F32),
            pltpu.VMEM((groups, 2 * width, span), BF16),
            pltpu.VMEM((small, span), F32),
        ],
        compiler_params=pltpu.CompilerParams(vmem_limit_bytes=40 << 20),
        name="mix",
    )(
        values, gate_in, write_proj, read_proj, step_size, log_gate, skip_gain,
        norm_gain.reshape(1, -1), entering,
    )
    return normed, final_state


def solution(mesh):
    rows = P(("batch", "seq"), "tp")
    return jax.shard_map(
        body,
        mesh=mesh,
        in_specs=(rows, rows, rows, rows, rows, rows, P("tp"), P("tp"), P(("batch", "tp"), None, None)),
        out_specs=(rows, P(("batch", "tp"), "seq", None)),
        check_vma=False,
    )
```

time: 146 us -> 39.5 us (0.27)
  local copies, waits for them, and re-layouts: 64.3 us -> 8.08 us
  matrix products: 45.1 us -> 0 us
  Pallas kernels: 0 us -> 30.4 us
  other arithmetic: 16.2 us -> 0 us
  between operations: 14.2 us -> 0.71 us
  starting transfers between devices: 4.75 us -> 0 us
    dot_general x5 -> x0, matrix products: 45.1 us -> none  [the longest x1 16.6 us: body(): jnp.einsum('gkpn,tgn->tgkp', entering, read_rows, precision=highest)]
    pallas_call x0 -> x2, Pallas kernels: none -> 30.4 us  [the longest x1 17.4 us: body(): pl.pallas_call(mix_kernel, grid=(rows // small,), in_specs=[pl.BlockSpec(...]
    reshape x8 -> x1, local copies, waits for them, and re-layouts: 29.6 us -> 0.75 us  [body(): norm_gain.reshape(1, -1)]
    unnamed x19 -> x15, local copies, waits for them, and re-layouts: 17.3 us -> 7.32 us
    add x1 -> x0, local copies, waits for them, and re-layouts: 8.08 us -> none  [body(): inside + earlier]
    convert_element_type x1 -> x0, local copies, waits for them, and re-layouts: 6.87 us -> none  [body(): inputs_flat = values.astype(jnp.float32)]
    ppermute x2 -> x0, starting transfers between devices: 4.72 us -> none  [shifted(): return lax.ppermute(array, axis, pairs)]
    another operation x4 -> x0, other arithmetic: 4.67 us -> none
  transfers between devices with their start and end apart: 3 -> 0, of which waited for: 0 -> 0; matrix products, arithmetic and copies ran while one was open for 78% -> 0% of each run, Pallas kernels for 0% -> 0%
where the time goes in v1:
time: 39.5 us; the launch traced here: 39.2 us
  Pallas kernels  30.4 us (77%)
  local copies, waits for them, and re-layouts  8.08 us (20%)
  between operations  0.71 us (2%)
    pallas_call x1, Pallas kernels, body(): pl.pallas_call(mix_kernel, grid=(rows // small,), in_specs=[pl.BlockSpec(...  17.4 us
    pallas_call x1, Pallas kernels, body(): pl.pallas_call(functools.partial(chain_kernel, peers), grid=(groups, rows...  13 us
    unnamed x15, local copies, waits for them, and re-layouts  7.32 us

profile of v1, /device:TPU:0, one launch (start us, length us, event | category | flops | bytes accessed | tf_op | source)
XLA Modules:
  0.0 39.2 jit_solution(10721198946383347945)
XLA Ops:
  0.6 0.0 copy-start.5
  0.6 0.0 copy-start.4
  0.7 0.8 %reshape.7.gain_ref = bf16[1,2048]{1,0:T(2,128)(2,1)S(1)} reshape(bf16[2048]{0:T(1024)(128)(2,1)} %param.16) | data formatting | bytes 8192 | tf_op jit(solution)/shard_map/reshape | solution.py:328
  1.4 1.0 %copy.13.step_ref = f32[1024,16]{1,0:T(8,128)S(1)} copy(f32[1024,16]{0,1:T(8,128)} %param.13) | data formatting | bytes 131072 | tf_op args[4]
  2.4 1.0 %copy.14.gate_ref = f32[1024,16]{1,0:T(8,128)S(1)} copy(f32[1024,16]{0,1:T(8,128)} %param.14) | data formatting | bytes 131072 | tf_op args[5]
  3.5 0.0 copy-start
  3.5 2.2 %copy-done = bf16[1024,2048]{1,0:T(8,128)(2,1)S(1)} copy-done((bf16[1024,2048]{1,0:T(8,128)(2,1)S(1)}, bf16[1024,2048]{1,0:T(8,128)(2,1)}, u32[]{:S(2)}) %copy-start) | copy-done | bytes 4194328
  5.7 0.0 copy-start.2
  5.7 1.0 %copy-done.2 = bf16[1024,256]{1,0:T(8,128)(2,1)S(1)} copy-done((bf16[1024,256]{1,0:T(8,128)(2,1)S(1)}, bf16[1024,256]{1,0:T(8,128)(2,1)}, u32[]{:S(2)}) %copy-start.2) | copy-done | bytes 524312
  6.7 0.0 copy-start.3
  6.7 1.2 %copy-done.3 = f32[16,128,128]{2,1,0:T(8,128)S(1)} copy-done((f32[16,128,128]{2,1,0:T(8,128)S(1)}, f32[16,128,128]{2,1,0:T(8,128)}, u32[]{:S(2)}) %copy-start.3) | copy-done | bytes 1048600
  7.9 0.0 copy-start.1
  8.0 13.0 %chain.1 = (f32[2,128,1024]{2,1,0:T(8,128)S(1)}, f32[16,64,128]{2,1,0:T(8,128)S(1)}) custom-call(bf16[1024,2048]{1,0:T(8,128)(2,1)S(1)} %copy-done, bf16[1024,256]{1,0:T(8,128)(2,1)S(1)} %copy-done.2, f32[1024,16]{1,0:T(8,128)S(1)} %copy.13.step_ref, f32[1024,16]{1,0:T(8,128)S(1)} %copy.14.gate_ref, f32[16,128,128]{2,1,0:T(8,128)S(1)} %copy-done.3), custom_call_target="tpu_custom_call" | custom-call | tf_op jit(solution)/shard_map/chain/pallas_call | solution.py:267
  21.0 0.0 copy-done.5
  21.0 0.0 copy-done.4
  21.0 0.0 copy-done.1
  21.0 17.4 %mix.1 = bf16[1024,2048]{1,0:T(8,128)(2,1)} custom-call(bf16[1024,2048]{1,0:T(8,128)(2,1)S(1)} %copy-done, bf16[1024,2048]{1,0:T(8,128)(2,1)S(1)} %copy-done.1, bf16[1024,256]{1,0:T(8,128)(2,1)S(1)} %copy-done.2, bf16[1024,256]{1,0:T(8,128)(2,1)S(1)} %copy-done.4, f32[1024,16]{1,0:T(8,128)S(1)} %copy.13.step_ref, f32[1024,16]{1,0:T(8,128)S(1)} %copy.14.gate_ref, ...), custom_call_target="tpu_custom_call" | custom-call | tf_op jit(solution)/shard_map/mix/pallas_call | solution.py:303
  38.4 0.8 %copy.16 = f32[16,64,128]{2,1,0:T(8,128)} copy(f32[16,64,128]{2,1,0:T(8,128)S(1)} %get-tuple-element.9) | data formatting | bytes 1048576
Async XLA Ops:
  0.6 20.3 %copy-start.5 = (f32[16]{0:T(128)S(1)}, f32[16]{0:T(128)}, u32[]{:S(2)}) copy-start(f32[16]{0:T(128)} %skip_ref.1) | copy-start | bytes 196
  0.6 20.3 %copy-start.4 = (bf16[1024,256]{1,0:T(8,128)(2,1)S(1)}, bf16[1024,256]{1,0:T(8,128)(2,1)}, u32[]{:S(2)}) copy-start(bf16[1024,256]{1,0:T(8,128)(2,1)} %c_ref.1) | copy-start | bytes 1572868
  3.5 2.2 %copy-start = (bf16[1024,2048]{1,0:T(8,128)(2,1)S(1)}, bf16[1024,2048]{1,0:T(8,128)(2,1)}, u32[]{:S(2)}) copy-start(bf16[1024,2048]{1,0:T(8,128)(2,1)} %x_ref.3) | copy-start | bytes 12582916
  5.7 1.0 %copy-start.2 = (bf16[1024,256]{1,0:T(8,128)(2,1)S(1)}, bf16[1024,256]{1,0:T(8,128)(2,1)}, u32[]{:S(2)}) copy-start(bf16[1024,256]{1,0:T(8,128)(2,1)} %b_ref.3) | copy-start | bytes 1572868
  6.7 1.2 %copy-start.3 = (f32[16,128,128]{2,1,0:T(8,128)S(1)}, f32[16,128,128]{2,1,0:T(8,128)}, u32[]{:S(2)}) copy-start(f32[16,128,128]{2,1,0:T(8,128)} %hist_ref.1) | copy-start | bytes 3145732
  7.9 13.0 %copy-start.1 = (bf16[1024,2048]{1,0:T(8,128)(2,1)S(1)}, bf16[1024,2048]{1,0:T(8,128)(2,1)}, u32[]{:S(2)}) copy-start(bf16[1024,2048]{1,0:T(8,128)(2,1)} %z_ref.1) | copy-start | bytes 12582916

commit v2 on v1

v2 whole, which is shorter than its diff:
```python
import functools
import math

import jax
import jax.numpy as jnp
from jax import lax
from jax.experimental import pallas as pl
from jax.experimental.pallas import tpu as pltpu
from jax.sharding import PartitionSpec as P

VMEM = 60 << 20
LOG2E = math.log2(math.e)
MESH = pl.DeviceIdType.MESH
F32 = jnp.float32
BF16 = jnp.bfloat16


def upper(size):
    rows = lax.broadcasted_iota(jnp.int32, (size, size), 0)
    cols = lax.broadcasted_iota(jnp.int32, (size, size), 1)
    return rows <= cols


def split(value):
    high = value.astype(BF16)
    low = (value - high.astype(F32)).astype(BF16)
    return high, low


def prefix_sums(rows):
    size = rows.shape[1]
    first = rows.astype(BF16)
    rest = rows - first.astype(F32)
    second = rest.astype(BF16)
    third = (rest - second.astype(F32)).astype(BF16)
    ones = upper(size).astype(BF16)
    return jnp.dot(
        jnp.concatenate([first, second, third], axis=1),
        jnp.concatenate([ones, ones, ones], axis=0),
        preferred_element_type=F32,
    )


def chain_kernel(
    peers, x_ref, b_ref, step_ref, gate_ref, hist_ref,
    ent_ref, fin_ref, shift_ref, last_ref, cols_ref,
    state, total, tails, recv, send, full, fin_recv,
    send_sem, recv_sem, fin_send_sem, fin_recv_sem,
):
    group, part = pl.program_id(0), pl.program_id(1)
    count, width, span = recv.shape
    blocks, heads, size = shift_ref.shape
    parts = b_ref.shape[0] // size
    steps = blocks // parts
    me = lax.axis_index("seq")
    per_group = heads // count
    share = fin_ref.shape[1]

    def peer(d):
        return dict(device_id={"seq": d}, device_id_type=MESH)

    @pl.when((group == 0) & (part == 0))
    def _():
        barrier = pltpu.get_barrier_semaphore()
        for by in range(1, peers):
            pl.semaphore_signal(barrier, inc=1, **peer(lax.rem(me + by, peers)))
        rows = [gate_ref[:, c * size : (c + 1) * size] for c in range(blocks)]
        cumul = prefix_sums(jnp.concatenate(rows, axis=0) * LOG2E)
        columns = jnp.transpose(cumul)
        after = jnp.zeros((heads, width), F32)
        for c in reversed(range(blocks)):
            here = cumul[c * heads : (c + 1) * heads]
            shift = here - jnp.log2(step_ref[:, c * size : (c + 1) * size])
            last = jnp.broadcast_to(here[:, size - 1 : size], (heads, width))
            shift_ref[c] = shift
            last_ref[c] = last
            cols_ref[c] = columns[:, c * heads : (c + 1) * heads]
            after = after + last
            tails[c] = jnp.exp2(after - shift)
        total[...] = jnp.exp2(after)

    turned_b = jnp.transpose(b_ref[...].astype(F32))

    def link(g):
        return pltpu.make_async_remote_copy(
            src_ref=send.at[g], dst_ref=recv.at[g],
            send_sem=send_sem.at[g], recv_sem=recv_sem.at[g],
            **peer(jnp.minimum(me + 1, peers - 1)),
        )

    def to_peer(d, g):
        return pltpu.make_async_remote_copy(
            src_ref=full.at[d, g], dst_ref=fin_recv.at[g],
            send_sem=fin_send_sem.at[d, g], recv_sem=fin_recv_sem.at[g],
            **peer(d),
        )

    for g in range(count):

        @pl.when(group == g)
        def _(g=g):
            @pl.when(part == 0)
            def _():
                state[g] = jnp.zeros((width, span), F32)

            for k in range(per_group):
                h = g * per_group + k
                cols = slice(k * width, (k + 1) * width)
                tail = jnp.concatenate(
                    [tails[part * parts + j, h : h + 1, :] for j in range(parts)], axis=1
                )
                left = jnp.concatenate(split(turned_b * tail), axis=0)
                both = jnp.dot(left, x_ref[:, cols], preferred_element_type=F32)
                state[g, :, cols] += both[:width] + both[width:]

            @pl.when(part == steps - 1)
            def _():
                if g == 0:
                    pl.semaphore_wait(pltpu.get_barrier_semaphore(), peers - 1)

                @pl.when(me == 0)
                def _():
                    for k in range(per_group):
                        h = g * per_group + k
                        cols = slice(k * width, (k + 1) * width)
                        entering = jnp.transpose(hist_ref[h])
                        ent_ref[g, :, cols] = entering
                        send[g, :, cols] = total[h : h + 1, :] * entering + state[g, :, cols]
                    link(g).start()

    @pl.when((group == count - 1) & (part == steps - 1))
    def _():
        @pl.when(me > 0)
        def _():
            for g in range(count):
                link(g).wait_recv()
                for k in range(per_group):
                    h = g * per_group + k
                    cols = slice(k * width, (k + 1) * width)
                    entering = recv[g, :, cols]
                    ent_ref[g, :, cols] = entering
                    send[g, :, cols] = total[h : h + 1, :] * entering + state[g, :, cols]

                @pl.when(me < peers - 1)
                def _(g=g):
                    link(g).start()

                @pl.when(me == peers - 1)
                def _(g=g):
                    for k in range(per_group):
                        cols = slice(k * width, (k + 1) * width)
                        closing = jnp.transpose(send[g, :, cols])
                        for d in range(peers - 1):
                            full[d, g, k] = closing[d * share : (d + 1) * share]
                        fin_ref[g * per_group + k] = closing[(peers - 1) * share :]
                    for d in range(peers - 1):
                        to_peer(d, g).start()

        @pl.when(me == peers - 1)
        def _():
            for g in range(count):
                for d in range(peers - 1):
                    to_peer(d, g).wait_send()

        @pl.when(me < peers - 1)
        def _():
            for g in range(count):
                link(g).wait_send()
            for g in range(count):
                to_peer(0, g).wait_recv()
                fin_ref[g * per_group : (g + 1) * per_group] = fin_recv[g]


def mix_kernel(
    x_ref, z_ref, b_ref, c_ref, skip_ref, gain_ref, ent_ref, shift_ref, last_ref, cols_ref,
    out_ref, state, parts, gated,
):
    groups, width, span = state.shape
    size = b_ref.shape[0]
    per_group = span // width

    @pl.when(pl.program_id(0) == 0)
    def _():
        for g in range(groups):
            for k in range(per_group):
                cols = slice(k * width, (k + 1) * width)
                entering = ent_ref[g, :, cols]
                high, low = split(entering)
                state[g, :, cols] = entering
                parts[g, :width, cols] = high
                parts[g, width:, cols] = low

    shift, last, cumul = shift_ref[0], last_ref[0], cols_ref[0]
    tails = jnp.exp2(last - shift)
    decays = jnp.exp2(last)
    rows = lax.broadcasted_iota(jnp.int32, (size, size), 0)
    cols_at = lax.broadcasted_iota(jnp.int32, (size, size), 1)
    causal = rows >= cols_at
    for g in range(groups):
        write = b_ref[:, g * width : (g + 1) * width]
        read = c_ref[:, g * width : (g + 1) * width]
        scores = lax.dot_general(
            read, write, (((1,), (1,)), ((), ())), preferred_element_type=F32
        )
        scores = jnp.where(causal, scores, 0.0)
        turned_b = jnp.transpose(write.astype(F32))
        earlier = jnp.dot(
            jnp.concatenate([read, read], axis=1), parts[g], preferred_element_type=F32
        )
        squares = jnp.zeros((size, width), F32)
        for k in range(per_group):
            h = g * per_group + k
            cols = slice(k * width, (k + 1) * width)
            wide = slice(h * width, (h + 1) * width)
            x = x_ref[:, wide]
            along = jnp.broadcast_to(cumul[:, h : h + 1], (size, width))
            weights = scores * jnp.exp2(jnp.minimum(along - shift[h : h + 1, :], 0.0))
            left = jnp.concatenate(
                [
                    jnp.concatenate(split(weights), axis=1),
                    jnp.concatenate(split(turned_b * tails[h : h + 1, :]), axis=1),
                ],
                axis=0,
            )
            both = jnp.dot(left, jnp.concatenate([x, x], axis=0), preferred_element_type=F32)
            later = decays[h : h + 1, :] * state[g, :, cols] + both[size:]
            high, low = split(later)
            state[g, :, cols] = later
            parts[g, :width, cols] = high
            parts[g, width:, cols] = low
            y = both[:size] + jnp.exp2(along) * earlier[:, cols] + skip_ref[h] * x.astype(F32)
            half = (0.5 * z_ref[:, wide]).astype(F32)
            value = y * half
            value = value + value * jnp.tanh(half)
            gated[:, cols] = value
            squares = squares + value * value
        mean = jnp.sum(squares, axis=1, keepdims=True) * (1.0 / span)
        scale = jnp.broadcast_to(lax.rsqrt(mean + 1e-05), (size, width))
        for k in range(per_group):
            h = g * per_group + k
            cols = slice(k * width, (k + 1) * width)
            wide = slice(h * width, (h + 1) * width)
            gain = gain_ref[pl.ds(h * width, width)].astype(F32).reshape(1, width)
            out_ref[:, wide] = (gated[:, cols] * scale * gain).astype(BF16)


def body(
    values, gate_in, write_proj, read_proj, step_size, log_gate, skip_gain, norm_gain, history
):
    heads, head_size, width = history.shape
    groups = write_proj.shape[1] // width
    per_group = heads // groups
    span = per_group * head_size
    rows = values.shape[0]
    peers = lax.axis_size("seq")
    share = head_size // peers
    size = math.gcd(rows, 128)
    blocks = rows // size
    big = math.gcd(rows, 512)

    def whole(*shape):
        return pl.BlockSpec(shape, lambda *_: (0,) * len(shape))

    entering, final_state, shifts, lasts, columns = pl.pallas_call(
        functools.partial(chain_kernel, peers),
        grid=(groups, rows // big),
        in_specs=[
            pl.BlockSpec((big, span), lambda g, c: (c, g)),
            pl.BlockSpec((big, width), lambda g, c: (c, g)),
            whole(heads, rows),
            whole(heads, rows),
            whole(heads, head_size, width),
        ],
        out_specs=[
            whole(groups, width, span),
            whole(heads, share, width),
            whole(blocks, heads, size),
            whole(blocks, heads, width),
            whole(blocks, size, heads),
        ],
        out_shape=[
            jax.ShapeDtypeStruct((groups, width, span), F32),
            jax.ShapeDtypeStruct((heads, share, width), F32),
            jax.ShapeDtypeStruct((blocks, heads, size), F32),
            jax.ShapeDtypeStruct((blocks, heads, width), F32),
            jax.ShapeDtypeStruct((blocks, size, heads), F32),
        ],
        scratch_shapes=[
            pltpu.VMEM((groups, width, span), F32),
            pltpu.VMEM((heads, width), F32),
            pltpu.VMEM((blocks, heads, size), F32),
            pltpu.VMEM((groups, width, span), F32),
            pltpu.VMEM((groups, width, span), F32),
            pltpu.VMEM((peers - 1, groups, per_group, share, width), F32),
            pltpu.VMEM((groups, per_group, share, width), F32),
            pltpu.SemaphoreType.DMA((groups,)),
            pltpu.SemaphoreType.DMA((groups,)),
            pltpu.SemaphoreType.DMA((peers - 1, groups)),
            pltpu.SemaphoreType.DMA((groups,)),
        ],
        compiler_params=pltpu.CompilerParams(
            collective_id=0, has_side_effects=True, vmem_limit_bytes=VMEM
        ),
        name="chain",
    )(values, write_proj, step_size.T, log_gate.T, history)

    normed = pl.pallas_call(
        mix_kernel,
        grid=(blocks,),
        in_specs=[
            pl.BlockSpec((size, heads * head_size), lambda c: (c, 0)),
            pl.BlockSpec((size, heads * head_size), lambda c: (c, 0)),
            pl.BlockSpec((size, groups * width), lambda c: (c, 0)),
            pl.BlockSpec((size, groups * width), lambda c: (c, 0)),
            pl.BlockSpec(memory_space=pltpu.SMEM),
            whole(heads * head_size),
            whole(groups, width, span),
            pl.BlockSpec((1, heads, size), lambda c: (c, 0, 0)),
            pl.BlockSpec((1, heads, width), lambda c: (c, 0, 0)),
            pl.BlockSpec((1, size, heads), lambda c: (c, 0, 0)),
        ],
        out_specs=pl.BlockSpec((size, heads * head_size), lambda c: (c, 0)),
        out_shape=jax.ShapeDtypeStruct((rows, heads * head_size), BF16),
        scratch_shapes=[
            pltpu.VMEM((groups, width, span), F32),
            pltpu.VMEM((groups, 2 * width, span), BF16),
            pltpu.VMEM((size, span), F32),
        ],
        compiler_params=pltpu.CompilerParams(vmem_limit_bytes=VMEM),
        name="mix",
    )(
        values, gate_in, write_proj, read_proj, skip_gain, norm_gain, entering,
        shifts, lasts, columns,
    )
    return normed, final_state


def solution(mesh):
    rows = P(("batch", "seq"), "tp")
    return jax.shard_map(
        body,
        mesh=mesh,
        in_specs=(rows, rows, rows, rows, rows, rows, P("tp"), P("tp"), P(("batch", "tp"), None, None)),
        out_specs=(rows, P(("batch", "tp"), "seq", None)),
        check_vma=False,
    )
```

time: 39.5 us -> 29.6 us (0.75)
  local copies, waits for them, and re-layouts: 8.08 us -> 0.8 us
  Pallas kernels: 30.4 us -> 27.7 us
    unnamed x15 -> x3, local copies, waits for them, and re-layouts: 7.32 us -> 0.8 us
    pallas_call x1, Pallas kernels: 13 us -> 11.3 us  [body(): pl.pallas_call(functools.partial(chain_kernel, peers), grid=(groups, rows...]
    pallas_call x1, Pallas kernels: 17.4 us -> 16.4 us  [body(): pl.pallas_call(mix_kernel, grid=(blocks,), in_specs=[pl.BlockSpec((size,...]
    reshape x1 -> x0, local copies, waits for them, and re-layouts: 0.75 us -> none  [body(): norm_gain.reshape(1, -1)]
where the time goes in v2:
time: 29.6 us; the launch traced here: 29.1 us
  Pallas kernels  27.7 us (94%)
  local copies, waits for them, and re-layouts  0.8 us (3%)
  between operations  0.65 us (2%)
    pallas_call x1, Pallas kernels, body(): pl.pallas_call(mix_kernel, grid=(blocks,), in_specs=[pl.BlockSpec((size,...  16.4 us
    pallas_call x1, Pallas kernels, body(): pl.pallas_call(functools.partial(chain_kernel, peers), grid=(groups, rows...  11.3 us
    unnamed x3, local copies, waits for them, and re-layouts  0.8 us

profile of v2, /device:TPU:0, one launch (start us, length us, event | category | flops | bytes accessed | tf_op | source)
XLA Modules:
  0.0 29.1 jit_solution(7289367825268704967)
XLA Ops:
  0.6 11.3 %chain.1 = (f32[2,128,1024]{2,1,0:T(8,128)}, f32[16,64,128]{2,1,0:T(8,128)}, f32[8,16,128]{2,1,0:T(8,128)}, f32[8,16,128]{2,1,0:T(8,128)}, f32[8,128,16]{2,1,0:T(8,128)}) custom-call(bf16[1024,2048]{1,0:T(8,128)(2,1)} %x_ref.3, bf16[1024,256]{1,0:T(8,128)(2,1)} %b_ref.3, f32[16,1024]{1,0:T(8,128)} %bitcast.2, f32[16,1024]{1,0:T(8,128)} %bitcast.3, ...), custom_call_target="tpu_custom_call" | custom-call | tf_op jit(solution)/shard_map/chain/pallas_call | solution.py:264
  11.9 0.0 copy-start
  11.9 16.4 %mix.1 = bf16[1024,2048]{1,0:T(8,128)(2,1)} custom-call(bf16[1024,2048]{1,0:T(8,128)(2,1)} %x_ref.3, bf16[1024,2048]{1,0:T(8,128)(2,1)} %z_ref.1, bf16[1024,256]{1,0:T(8,128)(2,1)} %b_ref.3, bf16[1024,256]{1,0:T(8,128)(2,1)} %c_ref.1, f32[16]{0:T(128)} %skip_ref.1, bf16[2048]{0:T(1024)(128)(2,1)} %gain_ref.1, f32[2,128,1024]{2,1,0:T(8,128)} %get-tuple-element.7.ent_ref, ...), custom_call_target="tpu_custom_call" | custom-call | tf_op jit(solution)/shard_map/mix/pallas_call | solution.py:307
  28.3 0.0 copy-done
  28.3 0.8 %copy.12 = f32[16,64,128]{2,1,0:T(8,128)} copy(f32[16,64,128]{2,1,0:T(8,128)S(1)} %copy-done) | data formatting | bytes 1048576
Async XLA Ops:
  11.9 16.4 %copy-start = (f32[16,64,128]{2,1,0:T(8,128)S(1)}, f32[16,64,128]{2,1,0:T(8,128)}, u32[]{:S(2)}) copy-start(f32[16,64,128]{2,1,0:T(8,128)} %get-tuple-element.15) | copy-start | bytes 1572868

commit v3 on v0

v3 whole, which is shorter than its diff:
```python
import functools
import math

import jax
import jax.numpy as jnp
from jax import lax
from jax.experimental import pallas as pl
from jax.experimental.pallas import tpu as pltpu
from jax.sharding import PartitionSpec as P

VMEM = 24 << 20
LOG2E = math.log2(math.e)
MESH = pl.DeviceIdType.MESH
F32 = jnp.float32
BF16 = jnp.bfloat16


def upper(size):
    rows = lax.broadcasted_iota(jnp.int32, (size, size), 0)
    cols = lax.broadcasted_iota(jnp.int32, (size, size), 1)
    return rows <= cols


def split(value):
    high = value.astype(BF16)
    low = (value - high.astype(F32)).astype(BF16)
    return high, low


def prefix_sums(rows):
    size = rows.shape[1]
    first = rows.astype(BF16)
    rest = rows - first.astype(F32)
    second = rest.astype(BF16)
    third = (rest - second.astype(F32)).astype(BF16)
    ones = upper(size).astype(BF16)
    return jnp.dot(
        jnp.concatenate([first, second, third], axis=1),
        jnp.concatenate([ones, ones, ones], axis=0),
        preferred_element_type=F32,
    )


def chain_kernel(
    peers, x_hbm, z_hbm, b_hbm, c_hbm, step_hbm, gate_hbm, hist_hbm, skip_hbm,
    fin_ref, ent_ref, delta_ref, y_ref, z_ref, c_ref, cols_ref, decay_ref,
    x_ref, b_ref, step_ref, gate_ref, hist_ref, skip_ref, shift_ref, tail_ref,
    state, total, recv, send, full, fin_recv,
    x_sem, z_sem, c_sem, b_sem, load_sem, send_sem, recv_sem, fin_send_sem, fin_recv_sem,
):
    count, width, span = recv.shape
    blocks, heads, size = shift_ref.shape
    me = lax.axis_index("seq")
    per_group = heads // count
    share = fin_ref.shape[1]

    def peer(d):
        return dict(device_id={"seq": d}, device_id_type=MESH)

    barrier = pltpu.get_barrier_semaphore()
    for by in range(1, peers):
        pl.semaphore_signal(barrier, inc=1, **peer(lax.rem(me + by, peers)))

    def block_copy(source, target, sem, c):
        return pltpu.make_async_copy(source.at[pl.ds(c * size, size)], target.at[c], sem.at[c])

    small = [
        pltpu.make_async_copy(gate_hbm, gate_ref, load_sem.at[0]),
        pltpu.make_async_copy(step_hbm, step_ref, load_sem.at[1]),
        pltpu.make_async_copy(hist_hbm, hist_ref, load_sem.at[2]),
        pltpu.make_async_copy(skip_hbm, skip_ref, load_sem.at[3]),
    ]
    small[0].start()
    small[1].start()
    for c in range(blocks):
        block_copy(b_hbm, b_ref, b_sem, c).start()
        block_copy(x_hbm, x_ref, x_sem, c).start()
    small[2].start()
    small[3].start()
    for c in range(blocks):
        block_copy(c_hbm, c_ref, c_sem, c).start()
    for c in range(blocks):
        block_copy(z_hbm, z_ref, z_sem, c).start()
    small[0].wait()
    small[1].wait()

    rows = [gate_ref[:, c * size : (c + 1) * size] for c in range(blocks)]
    cumul = prefix_sums(jnp.concatenate(rows, axis=0) * LOG2E)
    columns = jnp.transpose(cumul)
    after = jnp.zeros((heads, width), F32)
    for c in range(blocks):
        here = cumul[c * heads : (c + 1) * heads]
        shift = here - jnp.log2(step_ref[:, c * size : (c + 1) * size])
        last = jnp.broadcast_to(here[:, size - 1 : size], (heads, width))
        shift_ref[c] = shift
        cols_ref[c] = columns[:, c * heads : (c + 1) * heads]
        decay_ref[c] = jnp.exp2(last)
        tail_ref[c] = jnp.exp2(last - shift)
        after = after + last
    total[...] = jnp.exp2(after)
    state[...] = jnp.zeros_like(state)

    def gather(c, carry):
        block_copy(b_hbm, b_ref, b_sem, c).wait()
        block_copy(x_hbm, x_ref, x_sem, c).wait()
        tails, decays = tail_ref[c], decay_ref[c]
        for g in range(count):
            turned_b = jnp.transpose(b_ref[c, :, g * width : (g + 1) * width].astype(F32))
            for k in range(per_group):
                h = g * per_group + k
                cols = slice(k * width, (k + 1) * width)
                x = x_ref[c, :, h * width : (h + 1) * width]
                left = jnp.concatenate(split(turned_b * tails[h : h + 1, :]), axis=1)
                delta = jnp.dot(
                    left, jnp.concatenate([x, x], axis=0), preferred_element_type=F32
                )
                delta_ref[c, g, :, cols] = delta
                state[g, :, cols] = decays[h : h + 1, :] * state[g, :, cols] + delta
        return carry

    lax.fori_loop(0, blocks, gather, 0)

    def link(g):
        return pltpu.make_async_remote_copy(
            src_ref=send.at[g], dst_ref=recv.at[g],
            send_sem=send_sem.at[g], recv_sem=recv_sem.at[g],
            **peer(jnp.minimum(me + 1, peers - 1)),
        )

    def to_peer(d, g):
        return pltpu.make_async_remote_copy(
            src_ref=full.at[d, g], dst_ref=fin_recv.at[g],
            send_sem=fin_send_sem.at[d, g], recv_sem=fin_recv_sem.at[g],
            **peer(d),
        )

    def enter(g, k, entering):
        h = g * per_group + k
        cols = slice(k * width, (k + 1) * width)
        ent_ref[g, :, cols] = entering
        send[g, :, cols] = total[h : h + 1, :] * entering + state[g, :, cols]

    small[2].wait()
    small[3].wait()
    pl.semaphore_wait(barrier, peers - 1)

    @pl.when(me == 0)
    def _():
        for g in range(count):
            for k in range(per_group):
                enter(g, k, jnp.transpose(hist_ref[g * per_group + k]))
            link(g).start()

    causal = lax.broadcasted_iota(jnp.int32, (size, size), 0) >= lax.broadcasted_iota(
        jnp.int32, (size, size), 1
    )

    def within(c, carry):
        block_copy(c_hbm, c_ref, c_sem, c).wait()
        shift, cumul = shift_ref[c], cols_ref[c]
        for g in range(count):
            scores = lax.dot_general(
                c_ref[c, :, g * width : (g + 1) * width],
                b_ref[c, :, g * width : (g + 1) * width],
                (((1,), (1,)), ((), ())),
                preferred_element_type=F32,
            )
            scores = jnp.where(causal, scores, 0.0)
            for k in range(per_group):
                h = g * per_group + k
                wide = slice(h * width, (h + 1) * width)
                x = x_ref[c, :, wide]
                along = jnp.broadcast_to(cumul[:, h : h + 1], (size, size))
                weights = scores * jnp.exp2(jnp.minimum(along - shift[h : h + 1, :], 0.0))
                y_ref[c, :, wide] = skip_ref[h] * x.astype(F32) + jnp.dot(
                    jnp.concatenate(split(weights), axis=1),
                    jnp.concatenate([x, x], axis=0),
                    preferred_element_type=F32,
                )
        return carry

    middle = (blocks + 1) // 2
    lax.fori_loop(0, middle, within, 0)

    @pl.when(me > 0)
    def _():
        for g in range(count):
            link(g).wait_recv()
            for k in range(per_group):
                enter(g, k, recv[g, :, k * width : (k + 1) * width])

            @pl.when(me < peers - 1)
            def _(g=g):
                link(g).start()

            @pl.when(me == peers - 1)
            def _(g=g):
                for k in range(per_group):
                    closing = jnp.transpose(send[g, :, k * width : (k + 1) * width])
                    for d in range(peers - 1):
                        full[d, g, k] = closing[d * share : (d + 1) * share]
                    fin_ref[g * per_group + k] = closing[(peers - 1) * share :]
                for d in range(peers - 1):
                    to_peer(d, g).start()

    lax.fori_loop(middle, blocks, within, 0)
    for c in range(blocks):
        block_copy(z_hbm, z_ref, z_sem, c).wait()

    @pl.when(me == peers - 1)
    def _():
        for g in range(count):
            for d in range(peers - 1):
                to_peer(d, g).wait_send()

    @pl.when(me < peers - 1)
    def _():
        for g in range(count):
            link(g).wait_send()
        for g in range(count):
            to_peer(0, g).wait_recv()
            fin_ref[g * per_group : (g + 1) * per_group] = fin_recv[g]


def mix_kernel(
    gain_ref, ent_ref, delta_ref, y_ref, z_ref, c_ref, cols_ref, decay_ref,
    out_hbm, state, parts, gated, out_ref, out_sem,
):
    groups, width, span = state.shape
    blocks, size = c_ref.shape[:2]
    per_group = span // width

    for g in range(groups):
        for k in range(per_group):
            cols = slice(k * width, (k + 1) * width)
            entering = ent_ref[g, :, cols]
            high, low = split(entering)
            state[g, :, cols] = entering
            parts[g, :width, cols] = high
            parts[g, width:, cols] = low

    def out_copy(c):
        return pltpu.make_async_copy(
            out_ref.at[c], out_hbm.at[pl.ds(c * size, size)], out_sem.at[c]
        )

    def block(c, carry):
        cumul, decays = cols_ref[c], decay_ref[c]
        for g in range(groups):
            read = c_ref[c, :, g * width : (g + 1) * width]
            earlier = jnp.dot(
                jnp.concatenate([read, read], axis=1), parts[g], preferred_element_type=F32
            )
            squares = jnp.zeros((size, width), F32)
            for k in range(per_group):
                h = g * per_group + k
                cols = slice(k * width, (k + 1) * width)
                wide = slice(h * width, (h + 1) * width)
                later = decays[h : h + 1, :] * state[g, :, cols] + delta_ref[c, g, :, cols]
                high, low = split(later)
                state[g, :, cols] = later
                parts[g, :width, cols] = high
                parts[g, width:, cols] = low
                along = jnp.broadcast_to(cumul[:, h : h + 1], (size, width))
                y = y_ref[c, :, wide] + jnp.exp2(along) * earlier[:, cols]
                half = (0.5 * z_ref[c, :, wide]).astype(F32)
                value = y * half
                value = value + value * jnp.tanh(half)
                gated[:, cols] = value
                squares = squares + value * value
            mean = jnp.sum(squares, axis=1, keepdims=True) * (1.0 / span)
            scale = jnp.broadcast_to(lax.rsqrt(mean + 1e-05), (size, width))
            for k in range(per_group):
                h = g * per_group + k
                cols = slice(k * width, (k + 1) * width)
                wide = slice(h * width, (h + 1) * width)
                gain = gain_ref[pl.ds(h * width, width)].astype(F32).reshape(1, width)
                out_ref[c, :, wide] = (gated[:, cols] * scale * gain).astype(BF16)
        out_copy(c).start()
        return carry

    lax.fori_loop(0, blocks, block, 0)
    for c in range(blocks):
        out_copy(c).wait()


def body(
    values, gate_in, write_proj, read_proj, step_size, log_gate, skip_gain, norm_gain, history
):
    heads, head_size, width = history.shape
    groups = write_proj.shape[1] // width
    per_group = heads // groups
    span = per_group * head_size
    rows = values.shape[0]
    peers = lax.axis_size("seq")
    share = head_size // peers
    size = math.gcd(rows, 128)
    blocks = rows // size
    size = math.gcd(rows, 128)
    blocks = rows // size
    in_vmem = pl.BlockSpec(memory_space=pltpu.VMEM)
    in_hbm = pl.BlockSpec(memory_space=pltpu.HBM)
    dma = pltpu.SemaphoreType.DMA

    final_state, *handed = pl.pallas_call(
        functools.partial(chain_kernel, peers),
        in_specs=[in_hbm] * 8,
        out_specs=[in_vmem] * 8,
        out_shape=[
            jax.ShapeDtypeStruct((heads, share, width), F32),
            pltpu.VMEM((groups, width, span), F32),
            pltpu.VMEM((blocks, groups, width, span), F32),
            pltpu.VMEM((blocks, size, heads * head_size), F32),
            pltpu.VMEM((blocks, size, heads * head_size), BF16),
            pltpu.VMEM((blocks, size, groups * width), BF16),
            pltpu.VMEM((blocks, size, heads), F32),
            pltpu.VMEM((blocks, heads, width), F32),
        ],
        scratch_shapes=[
            pltpu.VMEM((blocks, size, heads * head_size), BF16),
            pltpu.VMEM((blocks, size, groups * width), BF16),
            pltpu.VMEM((heads, rows), F32),
            pltpu.VMEM((heads, rows), F32),
            pltpu.VMEM((heads, head_size, width), F32),
            pltpu.SMEM((heads,), F32),
            pltpu.VMEM((blocks, heads, size), F32),
            pltpu.VMEM((blocks, heads, size), F32),
            pltpu.VMEM((groups, width, span), F32),
            pltpu.VMEM((heads, width), F32),
            pltpu.VMEM((groups, width, span), F32),
            pltpu.VMEM((groups, width, span), F32),
            pltpu.VMEM((peers - 1, groups, per_group, share, width), F32),
            pltpu.VMEM((groups, per_group, share, width), F32),
            dma((blocks,)),
            dma((blocks,)),
            dma((blocks,)),
            dma((blocks,)),
            dma((4,)),
            dma((groups,)),
            dma((groups,)),
            dma((peers - 1, groups)),
            dma((groups,)),
        ],
        compiler_params=pltpu.CompilerParams(
            collective_id=0, has_side_effects=True, vmem_limit_bytes=VMEM
        ),
        name="chain",
    )(
        *(
            pltpu.with_memory_space_constraint(array, pltpu.HBM)
            for array in (
                values, gate_in, write_proj, read_proj, step_size.T, log_gate.T, history,
                skip_gain,
            )
        )
    )

    normed = pl.pallas_call(
        mix_kernel,
        in_specs=[in_vmem] * 8,
        out_specs=in_hbm,
        out_shape=jax.ShapeDtypeStruct((rows, heads * head_size), BF16),
        scratch_shapes=[
            pltpu.VMEM((groups, width, span), F32),
            pltpu.VMEM((groups, 2 * width, span), BF16),
            pltpu.VMEM((size, span), F32),
            pltpu.VMEM((blocks, size, heads * head_size), BF16),
            dma((blocks,)),
        ],
        compiler_params=pltpu.CompilerParams(vmem_limit_bytes=VMEM),
        name="mix",
    )(norm_gain, *handed)
    return normed, final_state


def solution(mesh):
    rows = P(("batch", "seq"), "tp")
    return jax.shard_map(
        body,
        mesh=mesh,
        in_specs=(rows, rows, rows, rows, rows, rows, P("tp"), P("tp"), P(("batch", "tp"), None, None)),
        out_specs=(rows, P(("batch", "tp"), "seq", None)),
        check_vma=False,
    )
```

time: 146 us -> 24.8 us (0.17)
  local copies, waits for them, and re-layouts: 64.3 us -> 0.8 us
  matrix products: 45.1 us -> 0 us
  Pallas kernels: 0 us -> 23 us
  other arithmetic: 16.2 us -> 0 us
  between operations: 14.2 us -> 0.66 us
  starting transfers between devices: 4.75 us -> 0 us
    dot_general x5 -> x0, matrix products: 45.1 us -> none  [the longest x1 16.6 us: body(): jnp.einsum('gkpn,tgn->tgkp', entering, read_rows, precision=highest)]
    reshape x8 -> x0, local copies, waits for them, and re-layouts: 29.6 us -> none  [the longest x1 9.94 us: body(): inputs_flat.reshape(blocks, block, groups, per_group, head_size)]
    pallas_call x0 -> x2, Pallas kernels: none -> 23 us  [the longest x1 14 us: body(): pl.pallas_call(functools.partial(chain_kernel, peers), in_specs=[in_hbm]...]
    unnamed x19 -> x3, local copies, waits for them, and re-layouts: 17.3 us -> 0.8 us
    add x1 -> x0, local copies, waits for them, and re-layouts: 8.08 us -> none  [body(): inside + earlier]
    convert_element_type x1 -> x0, local copies, waits for them, and re-layouts: 6.87 us -> none  [body(): inputs_flat = values.astype(jnp.float32)]
    ppermute x2 -> x0, starting transfers between devices: 4.72 us -> none  [shifted(): return lax.ppermute(array, axis, pairs)]
    another operation x4 -> x0, other arithmetic: 4.67 us -> none
  transfers between devices with their start and end apart: 3 -> 0, of which waited for: 0 -> 0; matrix products, arithmetic and copies ran while one was open for 78% -> 0% of each run, Pallas kernels for 0% -> 0%
where the time goes in v3:
time: 24.8 us; the launch traced here: 24.5 us
  Pallas kernels  23 us (93%)
  local copies, waits for them, and re-layouts  0.8 us (3%)
  between operations  0.66 us (3%)
    pallas_call x1, Pallas kernels, body(): pl.pallas_call(functools.partial(chain_kernel, peers), in_specs=[in_hbm]...  14 us
    pallas_call x1, Pallas kernels, body(): pl.pallas_call(mix_kernel, in_specs=[in_vmem] * 8, out_specs=in_hbm, out_...  8.97 us
    unnamed x3, local copies, waits for them, and re-layouts  0.8 us

profile of v3, /device:TPU:0, one launch (start us, length us, event | category | flops | bytes accessed | tf_op | source)
XLA Modules:
  0.0 24.5 jit_solution(17241889658435010282)
XLA Ops:
  0.6 0.0 copy-start
  0.6 14.0 %chain.1 = (f32[16,64,128]{2,1,0:T(8,128)S(1)}, f32[2,128,1024]{2,1,0:T(8,128)S(1)}, f32[8,2,128,1024]{3,2,1,0:T(8,128)S(1)}, f32[8,128,2048]{2,1,0:T(8,128)S(1)...) custom-call(bf16[1024,2048]{1,0:T(8,128)(2,1)} %x_hbm.1, ...), custom_call_target="tpu_custom_call" | custom-call | tf_op jit(solution)/shard_map/chain/pallas_call | solution.py:305
  14.7 0.0 copy-done
  14.7 9.0 %mix.1 = bf16[1024,2048]{1,0:T(8,128)(2,1)} custom-call(bf16[2048]{0:T(1024)(128)(2,1)S(1)} %copy-done, f32[2,128,1024]{2,1,0:T(8,128)S(1)} %get-tuple-element.10.ent_ref, f32[8,2,128,1024]{3,2,1,0:T(8,128)S(1)} %get-tuple-element.11.delta_ref, f32[8,128,2048]{2,1,0:T(8,128)S(1)} %get-tuple-element.12.y_ref, ...), custom_call_target="tpu_custom_call" | custom-call | tf_op jit(solution)/shard_map/mix/pallas_call | solution.py:358
  23.7 0.8 %copy.12 = f32[16,64,128]{2,1,0:T(8,128)} copy(f32[16,64,128]{2,1,0:T(8,128)S(1)} %get-tuple-element.21) | data formatting | bytes 1048576
Async XLA Ops:
  0.6 14.1 %copy-start = (bf16[2048]{0:T(1024)(128)(2,1)S(1)}, bf16[2048]{0:T(1024)(128)(2,1)}, u32[]{:S(2)}) copy-start(bf16[2048]{0:T(1024)(128)(2,1)} %gain_ref.1) | copy-start | bytes 12292

commit v4 on v3

--- a/solution.py
+++ b/solution.py
@@ -279,7 +279,7 @@
         out_copy(c).start()
         return carry
 
-    lax.fori_loop(0, blocks, block, 0)
+    lax.fori_loop(0, blocks, block, 0, unroll=2 if blocks % 2 == 0 else 1)
     for c in range(blocks):
         out_copy(c).wait()
 

time: 24.8 us -> 25.6 us (1.032)
  Pallas kernels: 23 us -> 23.8 us
    pallas_call x1, Pallas kernels: 8.97 us -> 9.76 us  [body(): pl.pallas_call(mix_kernel, in_specs=[in_vmem] * 8, out_specs=in_hbm, out_...]
where the time goes in v4:
time: 25.6 us; the launch traced here: 25.3 us
  Pallas kernels  23.8 us (93%)
  local copies, waits for them, and re-layouts  0.8 us (3%)
  between operations  0.66 us (3%)
    pallas_call x1, Pallas kernels, body(): pl.pallas_call(functools.partial(chain_kernel, peers), in_specs=[in_hbm]...  14 us
    pallas_call x1, Pallas kernels, body(): pl.pallas_call(mix_kernel, in_specs=[in_vmem] * 8, out_specs=in_hbm, out_...  9.76 us
    unnamed x3, local copies, waits for them, and re-layouts  0.8 us

profile of v4, /device:TPU:0, one launch (start us, length us, event | category | flops | bytes accessed | tf_op | source)
XLA Modules:
  0.0 25.3 jit_solution(12346791568653956912)
XLA Ops:
  0.6 0.0 copy-start
  0.6 14.0 %chain.1 = (f32[16,64,128]{2,1,0:T(8,128)S(1)}, f32[2,128,1024]{2,1,0:T(8,128)S(1)}, f32[8,2,128,1024]{3,2,1,0:T(8,128)S(1)}, f32[8,128,2048]{2,1,0:T(8,128)S(1)...) custom-call(bf16[1024,2048]{1,0:T(8,128)(2,1)} %x_hbm.1, ...), custom_call_target="tpu_custom_call" | custom-call | tf_op jit(solution)/shard_map/chain/pallas_call | solution.py:305
  14.7 0.0 copy-done
  14.7 9.8 %mix.1 = bf16[1024,2048]{1,0:T(8,128)(2,1)} custom-call(bf16[2048]{0:T(1024)(128)(2,1)S(1)} %copy-done, f32[2,128,1024]{2,1,0:T(8,128)S(1)} %get-tuple-element.10.ent_ref, f32[8,2,128,1024]{3,2,1,0:T(8,128)S(1)} %get-tuple-element.11.delta_ref, f32[8,128,2048]{2,1,0:T(8,128)S(1)} %get-tuple-element.12.y_ref, ...), custom_call_target="tpu_custom_call" | custom-call | tf_op jit(solution)/shard_map/mix/pallas_call | solution.py:358
  24.5 0.8 %copy.12 = f32[16,64,128]{2,1,0:T(8,128)} copy(f32[16,64,128]{2,1,0:T(8,128)S(1)} %get-tuple-element.21) | data formatting | bytes 1048576
Async XLA Ops:
  0.6 14.1 %copy-start = (bf16[2048]{0:T(1024)(128)(2,1)S(1)}, bf16[2048]{0:T(1024)(128)(2,1)}, u32[]{:S(2)}) copy-start(bf16[2048]{0:T(1024)(128)(2,1)} %gain_ref.1) | copy-start | bytes 12292
